TPU v7x, 32 devices: a whole 2x2x4 slice. The times are simulated.
32 devices in a mesh: dp: 8 (over z, y), seq: 4 (over x, core).
Axes of the slice: x: 2, y: 2, z: 4, core: 2. Of those that a mesh axis runs over, the one named last changes fastest.
Arguments:
- hidden: bfloat16 [16, 2048, 768], P('dp', 'seq'), may hold values from -6 to 6
- lengths: int32 [16], P('dp'), may hold values from 512 to 2048
- norm_gain: float32 [768], P(('dp', 'seq')), may hold values from 0.5 to 1.5
- in_weight: float32 [768, 3352], P(('dp', 'seq')), may hold values from -0.21875 to 0.21875
- conv_weight: float32 [4, 1792], P(None, ('dp', 'seq')), may hold values from -3 to 3
- conv_bias: float32 [1792], P(('dp', 'seq')), may hold values from -2.5 to 2.5
- step_bias: float32 [24], replicated, may hold values from -10 to -5
- decay_log: float32 [24], replicated, may hold values from 0 to 1
- skip_gain: float32 [24], replicated, may hold values from 0.5 to 1.5
- gate_gain: float32 [1536], P(('dp', 'seq')), may hold values from 0.5 to 1.5
- out_weight: float32 [1536, 768], P(('dp', 'seq')), may hold values from -0.15625 to 0.15625
- cotangent: bfloat16 [16, 2048, 768], P('dp', 'seq'), may hold values from -6 to 6
Outputs:
- output: bfloat16 [16, 2048, 768], P('dp', 'seq')
- grad_hidden: bfloat16 [16, 2048, 768], P('dp', 'seq')
- grad_norm_gain: float32 [768], P(('dp', 'seq'))
- grad_in_weight: float32 [768, 3352], P(('dp', 'seq'))
- grad_conv_weight: float32 [4, 1792], P(None, ('dp', 'seq'))
- grad_conv_bias: float32 [1792], P(('dp', 'seq'))
- grad_step_bias: float32 [24], replicated
- grad_decay_log: float32 [24], replicated
- grad_skip_gain: float32 [24], replicated
- grad_gate_gain: float32 [1536], P(('dp', 'seq'))
- grad_out_weight: float32 [1536, 768], P(('dp', 'seq'))
All inputs are finite; a program needn't handle non-finite values.
Results may differ from a plain program's by a relative error of at most 0.00435.
The roundings to bfloat16 on the way count: a program that leaves them out, or rounds other values in their place, can miss the bound.
Values may be sent and summed in bfloat16 or wider, within the bound.
No kernel may reach another device: no remote copies, remote signals or barrier semaphores. Data moves between devices by JAX's collectives and lax.ppermute only.
A program may use at most 192 MiB of HBM per device.

v0:
```python
import jax
import jax.numpy as jnp
from jax import lax
from jax.sharding import PartitionSpec as P

H = 24
P_SIZE = 64
N = 128
KW = 4
Q = 256
DI = 1536
CD = 1792
epsilon = 1e-05


def from_behind(block, axis, distance):
    devices = range(lax.axis_size(axis))
    route = [(i - distance, i) for i in devices if i - distance in devices]
    return lax.ppermute(block, axis, route)


def rms_scale(values):
    return lax.rsqrt(jnp.mean(values * values, axis=-1, keepdims=True) + epsilon)


def decay_matrix(cum_group):
    width_q = cum_group.shape[-1]
    lower = jnp.arange(width_q)[:, None] >= jnp.arange(width_q)[None, :]
    gap = jnp.where(lower[None], cum_group[:, :, None] - cum_group[:, None, :], 0.0)
    return jnp.where(lower[None], jnp.exp(gap), 0.0)


def intra_forward(group_item):
    x_group, b_group, c_group, step_group, cum_group = group_item
    scores = jnp.einsum("qn,rn->qr", c_group, b_group, preferred_element_type=jnp.float32)
    mixing = (scores[None] * decay_matrix(cum_group) * step_group[:, None, :]).astype(jnp.bfloat16)
    return jnp.einsum("hqr,rhp->qhp", mixing, x_group, preferred_element_type=jnp.float32)


def intra_backward(group_item):
    x_group, b_group, c_group, step_group, cum_group, grad_group = group_item
    scores = jnp.einsum("qn,rn->qr", c_group, b_group, preferred_element_type=jnp.float32)
    spread = decay_matrix(cum_group)
    rate_weight = spread * step_group[:, None, :]
    mixing = (scores[None] * rate_weight).astype(jnp.bfloat16)
    grad_mixing = jnp.einsum(
        "qhp,rhp->hqr", grad_group, x_group, preferred_element_type=jnp.float32
    )
    grad_x = jnp.einsum("hqr,qhp->rhp", mixing, grad_group, preferred_element_type=jnp.float32)
    grad_scores = jnp.sum(grad_mixing * rate_weight, axis=0).astype(jnp.bfloat16)
    grad_c = jnp.einsum("qr,rn->qn", grad_scores, b_group, preferred_element_type=jnp.float32)
    grad_b = jnp.einsum("qr,qn->rn", grad_scores, c_group, preferred_element_type=jnp.float32)
    through = grad_mixing * scores[None] * spread
    cum_flow = through * step_group[:, None, :]
    grad_cum = jnp.sum(cum_flow, axis=2) - jnp.sum(cum_flow, axis=1)
    return (grad_x, grad_b, grad_c, jnp.sum(through, axis=1), grad_cum)


def per_device(
    hidden,
    lengths,
    norm_gain,
    in_weight,
    conv_weight,
    conv_bias,
    step_bias,
    decay_log,
    skip_gain,
    gate_gain,
    out_weight,
    cotangent,
):
    seq_count, piece_len, model_width = hidden.shape
    group_count = piece_len // Q
    block_count = seq_count * group_count
    token_rows = seq_count * piece_len
    halo_width = KW - 1
    shards = (
        norm_gain.astype(jnp.bfloat16),
        in_weight.astype(jnp.bfloat16),
        conv_weight.astype(jnp.bfloat16),
        conv_bias.astype(jnp.bfloat16),
        gate_gain.astype(jnp.bfloat16),
        out_weight.astype(jnp.bfloat16),
    )
    gathered = (
        lax.all_gather(shards[0], ("dp", "seq"), axis=0, tiled=True),
        lax.all_gather(shards[1], ("dp", "seq"), axis=0, tiled=True),
        lax.all_gather(shards[2], ("dp", "seq"), axis=1, tiled=True),
        lax.all_gather(shards[3], ("dp", "seq"), axis=0, tiled=True),
        lax.all_gather(shards[4], ("dp", "seq"), axis=0, tiled=True),
        lax.all_gather(shards[5], ("dp", "seq"), axis=0, tiled=True),
    )
    gain_in, in_full, kernel_full, bias_full, gain_gate, out_full = gathered
    positions = lax.axis_index("seq") * piece_len + jnp.arange(piece_len, dtype=jnp.int32)
    valid_mask = (positions[None, :] < lengths[:, None]).astype(jnp.float32)
    x_float = hidden.astype(jnp.float32)
    scale_in = rms_scale(x_float)
    normed = (
        (x_float * scale_in * gain_in.astype(jnp.float32))
        .astype(jnp.bfloat16)
        .reshape(token_rows, model_width)
    )
    projected = jnp.dot(normed, in_full, preferred_element_type=jnp.float32).reshape(
        seq_count, piece_len, -1
    )
    gate_z = projected[..., :DI]
    conv_in = projected[..., DI : DI + CD].astype(jnp.bfloat16)
    dt_raw = projected[..., DI + CD :]
    rim_rows = from_behind(conv_in[:, piece_len - halo_width :, :], "seq", 1)
    extended = jnp.concatenate([rim_rows, conv_in], axis=1)
    kernel = kernel_full.astype(jnp.float32)
    pre_act = bias_full.astype(jnp.float32) + sum(
        (
            kernel[offset] * extended[:, offset : offset + piece_len].astype(jnp.float32)
            for offset in range(KW)
        )
    )
    conv_out = jax.nn.silu(pre_act)
    x_heads = conv_out[..., :DI].astype(jnp.bfloat16).reshape(block_count, Q, H, P_SIZE)
    b_rows = conv_out[..., DI : DI + N].astype(jnp.bfloat16).reshape(block_count, Q, N)
    c_rows = conv_out[..., DI + N :].astype(jnp.bfloat16).reshape(block_count, Q, N)
    step_size = jax.nn.softplus(dt_raw + step_bias)
    decay_rate = jnp.exp(decay_log)
    step_blocks = step_size.reshape(block_count, Q, H).transpose(0, 2, 1)
    cum_decay = jnp.cumsum(-step_blocks * decay_rate[None, :, None], axis=2)
    intra_out = lax.map(intra_forward, (x_heads, b_rows, c_rows, step_blocks, cum_decay))
    tail_weight = jnp.exp(cum_decay[:, :, -1:] - cum_decay) * step_blocks
    b_scaled = (b_rows[:, None].astype(jnp.float32) * tail_weight[..., None]).astype(jnp.bfloat16)
    local_state = jnp.einsum(
        "bhqn,bqhp->bhnp", b_scaled, x_heads, preferred_element_type=jnp.float32
    )
    block_decay = jnp.exp(cum_decay[:, :, -1])
    group_decay = block_decay.reshape(seq_count, group_count, H)
    local_parts = local_state.reshape(seq_count, group_count, H, N, P_SIZE)
    running = jnp.zeros((seq_count, H, N, P_SIZE), jnp.float32)
    carried = jnp.ones((seq_count, H), jnp.float32)
    start_list = []
    prefix_list = []
    for block_index in range(group_count):
        start_list.append(running)
        prefix_list.append(carried)
        running = group_decay[:, block_index, :, None, None] * running + local_parts[:, block_index]
        carried = carried * group_decay[:, block_index]
    incoming = jnp.zeros_like(running)
    for rounds in range(lax.axis_size("seq") - 1):
        incoming = from_behind(carried[:, :, None, None] * incoming + running, "seq", 1)
    group_starts = jnp.stack(
        [
            start_list[block_index] + prefix_list[block_index][:, :, None, None] * incoming
            for block_index in range(group_count)
        ],
        axis=1,
    ).reshape(block_count, H, N, P_SIZE)
    growth = jnp.exp(cum_decay)
    c_scaled = c_rows[:, None].astype(jnp.float32) * growth[..., None]
    c_low = c_scaled.astype(jnp.bfloat16)
    starts_low = group_starts.astype(jnp.bfloat16)
    inter_out = jnp.einsum("bhqn,bhnp->bqhp", c_low, starts_low, preferred_element_type=jnp.float32)
    ssm_out = (
        intra_out + inter_out + skip_gain[None, None, :, None] * x_heads.astype(jnp.float32)
    ).reshape(seq_count, piece_len, DI)
    gate_sig = jax.nn.sigmoid(gate_z)
    gated_out = ssm_out * gate_z * gate_sig
    scale_gate = rms_scale(gated_out)
    gated_norm = (
        (gated_out * scale_gate * gain_gate.astype(jnp.float32))
        .astype(jnp.bfloat16)
        .reshape(token_rows, DI)
    )
    branch = jnp.dot(gated_norm, out_full, preferred_element_type=jnp.float32).reshape(
        seq_count, piece_len, model_width
    )
    output = (x_float + valid_mask[..., None] * branch).astype(jnp.bfloat16)
    back_shards = (shards[0], shards[1], shards[2], shards[4], shards[5])
    back_weights = (
        lax.all_gather(back_shards[0], ("dp", "seq"), axis=0, tiled=True),
        lax.all_gather(back_shards[1], ("dp", "seq"), axis=0, tiled=True),
        lax.all_gather(back_shards[2], ("dp", "seq"), axis=1, tiled=True),
        lax.all_gather(back_shards[3], ("dp", "seq"), axis=0, tiled=True),
        lax.all_gather(back_shards[4], ("dp", "seq"), axis=0, tiled=True),
    )
    gain_in_back, in_back, kernel_back, gain_gate_back, out_back = back_weights
    d_branch = (
        (cotangent.astype(jnp.float32) * valid_mask[..., None])
        .astype(jnp.bfloat16)
        .reshape(token_rows, model_width)
    )
    grad_out = jnp.einsum("tk,td->kd", gated_norm, d_branch, preferred_element_type=jnp.float32)
    grad_norm_out = jnp.einsum(
        "td,kd->tk", d_branch, out_back, preferred_element_type=jnp.float32
    ).reshape(seq_count, piece_len, DI)
    grad_gate_gain = jnp.sum(grad_norm_out * gated_out * scale_gate, axis=(0, 1))
    scaled_back = grad_norm_out * gain_gate_back.astype(jnp.float32)
    grad_gated = scale_gate * scaled_back - gated_out * (
        scale_gate * scale_gate * scale_gate
    ) * jnp.mean(scaled_back * gated_out, axis=-1, keepdims=True)
    grad_ssm = (grad_gated * gate_z * gate_sig).astype(jnp.bfloat16)
    grad_gate_z = grad_gated * ssm_out * gate_sig * (1.0 + gate_z * (1.0 - gate_sig))
    grad_blocks = grad_ssm.reshape(block_count, Q, H, P_SIZE)
    grad_skip = jnp.einsum("bqhp,bqhp->h", grad_blocks, x_heads, preferred_element_type=jnp.float32)
    intra_x, intra_b, intra_c, intra_step, intra_cum = lax.map(
        intra_backward, (x_heads, b_rows, c_rows, step_blocks, cum_decay, grad_blocks)
    )
    grad_in_y = jnp.einsum(
        "bhqn,bqhp->bhnp", c_low, grad_blocks, preferred_element_type=jnp.float32
    ).reshape(seq_count, group_count, H, N, P_SIZE)
    back_running = jnp.zeros((seq_count, H, N, P_SIZE), jnp.float32)
    for block_index in reversed(range(group_count)):
        back_running = (
            group_decay[:, block_index, :, None, None] * back_running + grad_in_y[:, block_index]
        )
    arriving = jnp.zeros_like(back_running)
    for rounds in range(lax.axis_size("seq") - 1):
        arriving = from_behind(carried[:, :, None, None] * arriving + back_running, "seq", -1)
    end_list = [None] * group_count
    following = arriving
    for block_index in reversed(range(group_count)):
        end_list[block_index] = following
        following = (
            group_decay[:, block_index, :, None, None] * following + grad_in_y[:, block_index]
        )
    grad_end = jnp.stack(end_list, axis=1).reshape(block_count, H, N, P_SIZE)
    grad_last = jnp.sum(grad_end * group_starts, axis=(2, 3)) * block_decay
    grad_local = grad_end.astype(jnp.bfloat16)
    grad_b_scaled = jnp.einsum(
        "bqhp,bhnp->bhqn", x_heads, grad_local, preferred_element_type=jnp.float32
    )
    grad_x_heads = (
        skip_gain[None, None, :, None] * grad_blocks.astype(jnp.float32)
        + intra_x
        + jnp.einsum("bhqn,bhnp->bqhp", b_scaled, grad_local, preferred_element_type=jnp.float32)
    )
    grad_b = intra_b + jnp.einsum("bhqn,bhq->bqn", grad_b_scaled, tail_weight)
    grad_tail = jnp.einsum("bhqn,bqn->bhq", grad_b_scaled, b_rows.astype(jnp.float32))
    tail_flow = grad_tail * tail_weight
    grad_step = intra_step + grad_tail * jnp.exp(cum_decay[:, :, -1:] - cum_decay)
    grad_c_scaled = jnp.einsum(
        "bqhp,bhnp->bhqn", grad_blocks, starts_low, preferred_element_type=jnp.float32
    )
    grad_c = intra_c + jnp.einsum("bhqn,bhq->bqn", grad_c_scaled, growth)
    grad_cum = intra_cum - tail_flow + jnp.einsum("bhqn,bhqn->bhq", grad_c_scaled, c_scaled)
    grad_cum = grad_cum.at[:, :, -1].add(grad_last + jnp.sum(tail_flow, axis=2))
    grad_log = lax.cumsum(grad_cum, axis=2, reverse=True)
    grad_step = grad_step - grad_log * decay_rate[None, :, None]
    grad_decay = -jnp.sum(grad_log * step_blocks, axis=(0, 2)) * decay_rate
    grad_step_tokens = grad_step.transpose(0, 2, 1).reshape(seq_count, piece_len, H)
    grad_dt_raw = grad_step_tokens * jax.nn.sigmoid(dt_raw + step_bias)
    grad_step_bias = jnp.sum(grad_dt_raw, axis=(0, 1))
    grad_conv_out = jnp.concatenate(
        [
            grad_x_heads.reshape(seq_count, piece_len, DI),
            grad_b.reshape(seq_count, piece_len, N),
            grad_c.reshape(seq_count, piece_len, N),
        ],
        axis=-1,
    )
    pre_sig = jax.nn.sigmoid(pre_act)
    grad_pre = grad_conv_out * pre_sig * (1.0 + pre_act * (1.0 - pre_sig))
    grad_conv_bias = jnp.sum(grad_pre, axis=(0, 1))
    grad_kernel = jnp.stack(
        [
            jnp.sum(
                grad_pre * extended[:, offset : offset + piece_len].astype(jnp.float32), axis=(0, 1)
            )
            for offset in range(KW)
        ],
        axis=0,
    )
    kernel_float = kernel_back.astype(jnp.float32)
    grad_ext = sum(
        (
            jnp.pad(
                kernel_float[offset] * grad_pre, ((0, 0), (offset, halo_width - offset), (0, 0))
            )
            for offset in range(KW)
        )
    )
    returned = from_behind(grad_ext[:, :halo_width].astype(jnp.bfloat16), "seq", -1).astype(
        jnp.float32
    )
    grad_conv_in = grad_ext[:, halo_width:] + jnp.pad(
        returned, ((0, 0), (piece_len - halo_width, 0), (0, 0))
    )
    grad_proj = (
        jnp.concatenate([grad_gate_z, grad_conv_in, grad_dt_raw], axis=-1)
        .astype(jnp.bfloat16)
        .reshape(token_rows, -1)
    )
    grad_in = jnp.einsum("td,te->de", normed, grad_proj, preferred_element_type=jnp.float32)
    grad_normed = jnp.einsum(
        "te,de->td", grad_proj, in_back, preferred_element_type=jnp.float32
    ).reshape(seq_count, piece_len, model_width)
    grad_norm_gain = jnp.sum(grad_normed * x_float * scale_in, axis=(0, 1))
    scaled_in = grad_normed * gain_in_back.astype(jnp.float32)
    grad_x_in = scale_in * scaled_in - x_float * (scale_in * scale_in * scale_in) * jnp.mean(
        scaled_in * x_float, axis=-1, keepdims=True
    )
    grad_hidden = (cotangent.astype(jnp.float32) + grad_x_in).astype(jnp.bfloat16)
    owned_grads = (
        lax.psum_scatter(grad_norm_gain, ("dp", "seq"), scatter_dimension=0, tiled=True),
        lax.psum_scatter(grad_in, ("dp", "seq"), scatter_dimension=0, tiled=True),
        lax.psum_scatter(grad_kernel, ("dp", "seq"), scatter_dimension=1, tiled=True),
        lax.psum_scatter(grad_conv_bias, ("dp", "seq"), scatter_dimension=0, tiled=True),
        lax.psum_scatter(grad_gate_gain, ("dp", "seq"), scatter_dimension=0, tiled=True),
        lax.psum_scatter(grad_out, ("dp", "seq"), scatter_dimension=0, tiled=True),
    )
    head_totals = lax.psum((grad_step_bias, grad_decay, grad_skip), ("dp", "seq"))
    return (
        output,
        grad_hidden,
        owned_grads[0],
        owned_grads[1],
        owned_grads[2],
        owned_grads[3],
        head_totals[0],
        head_totals[1],
        head_totals[2],
        owned_grads[4],
        owned_grads[5],
    )


def solution(mesh):
    return jax.shard_map(
        per_device,
        mesh=mesh,
        in_specs=(
            P("dp", "seq", None),
            P("dp"),
            P(("dp", "seq")),
            P(("dp", "seq"), None),
            P(None, ("dp", "seq")),
            P(("dp", "seq")),
            P(),
            P(),
            P(),
            P(("dp", "seq")),
            P(("dp", "seq"), None),
            P("dp", "seq", None),
        ),
        out_specs=(
            P("dp", "seq", None),
            P("dp", "seq", None),
            P(("dp", "seq")),
            P(("dp", "seq"), None),
            P(None, ("dp", "seq")),
            P(("dp", "seq")),
            P(),
            P(),
            P(),
            P(("dp", "seq")),
            P(("dp", "seq"), None),
        ),
        check_vma=False,
    )
```

profile of v0, /device:TPU:0, one launch (start us, length us, event | category | flops | bytes accessed | tf_op | source)
XLA Modules:
  0.0 762.1 jit_solution(16280473056816043643)
XLA Ops:
  12.2 42.3 %all-reduce.14 = (bf16[768]{0:T(1024)(128)(2,1)S(1)}, bf16[1792]{0:T(1024)(128)(2,1)S(1)}, bf16[1536]{0:T(1024)(128)(2,1)S(1)}) all-reduce(bf16[768]{0:T(1024)(128)(2,1)S(1)} %dynamic-update-slice.4, bf16[1792]{0:T(1024)(128)(2,1)S(1)} %dynamic-update-slice.3, ...), channel_id=1, replica_groups=mesh['dp'=8,'seq'=4] {'dp','seq'}, use_global_device_ids=true, to_apply=%add.6 | all-reduce | flops 4096 | bytes 16384
  55.2 40.5 %all-gather = bf16[32,56,4]{1,2,0:T(4,128)(2,1)S(1)} all-gather(bf16[1,56,4]{1,2,0:T(4,128)(2,1)S(1)} %convert_bitcast_fusion), channel_id=1, replica_groups=mesh['dp'=8,'seq'=4] {'dp','seq'}, dimensions={0}, use_global_device_ids=true | all-gather | bytes 14784 | tf_op jit(solution)/shard_map/all_gather | solution.py:89
  98.4 12.8 %fusion.145 = (bf16[2,512,3352]{1,2,0:T(8,128)(2,1)}, f32[2,512,3352]{1,2,0:T(8,128)}) fusion(bf16[768,3352]{1,0:T(8,128)(2,1)} %all-gather.4.cloned.1.call-done, bf16[2,512,768]{2,1,0:T(8,128)(2,1)} %param.18, f32[768]{0:T(1024)S(1)} %convert_element_type.157, f32[2,512]{1,0:T(2,128)S(1)} %get-tuple-element.308), kind=kOutput, calls=%fused_computation.256 | convolution fusion | flops 5278818304 | bytes 27323392 | tf_op jit(solution)/shard_map/dot_general | solution.py:104
  127.4 12.4 %multiply_convert_fusion.14 = (bf16[2,512,1792]{1,2,0:T(8,128)(2,1)S(1)}, f32[2,512,1792]{1,2,0:T(8,128)}) fusion(bf16[2,512,1792]{1,2,0:T(8,128)(2,1)} %slice.154, f32[1792]{0:T(1024)S(1)} %get-tuple-element.225, bf16[2,3,1792]{1,2,0:T(8,128)(2,1)S(1)} %copy.159, f32[1792]{0:T(1024)S(1)} %get-tuple-element.226, f32[1792]{0:T(1024)S(1)} %get-tuple-element.227, ...), kind=kLoop, calls=%fused_computation.107 | loop fusion | flops 47710208 | bytes 14737408 | tf_op jit(solution)/shard_map/convert.8
  140.9 14.5 %copy.160 = bf16[2,512,1536]{1,0,2:T(2,128)(2,1)} copy(bf16[2,512,1536]{1,2,0:T(8,128)(2,1)S(1)} %slice.162) | data formatting | bytes 6291456 | tf_op jit(solution)/shard_map/slice | solution.py:120
  155.3 7.4 reshape.307
  176.1 17.4 %collective-permute-start.2 = (f32[2,24,128,64]{2,3,1,0:T(8,128)}, f32[2,24,128,64]{2,3,1,0:T(8,128)}, u32[]{:S(2)}, u32[]{:S(2)}) collective-permute-start(f32[2,24,128,64]{2,3,1,0:T(8,128)} %multiply_add_fusion.3), channel_id=1, source_target_pairs={{0,1},{1,2},{2,3},{4,5},{5,6},{6,7},{8,9},{9,10},{10,11},{12,13},{... | collective-permute-start | bytes 4718600 | tf_op jit(solution)/shard_map/ppermute | solution.py:19
  203.8 15.6 %collective-permute-start.3 = (f32[2,24,128,64]{2,3,1,0:T(8,128)}, f32[2,24,128,64]{2,3,1,0:T(8,128)}, u32[]{:S(2)}, u32[]{:S(2)}) collective-permute-start(f32[2,24,128,64]{2,3,1,0:T(8,128)} %multiply_add_fusion.2), channel_id=1, source_target_pairs={{0,1},{1,2},{2,3},{4,5},{5,6},{6,7},{8,9},{9,10},{10,11},{12,13},{... | collective-permute-start | bytes 4718600 | tf_op jit(solution)/shard_map/ppermute | solution.py:19
  222.9 25.0 %while.29 = (s32[]{:T(128)}, f32[4,256,24,64]{1,3,2,0:T(8,128)}, bf16[4,256,24,64]{1,3,2,0:T(8,128)(2,1)}, bf16[4,256,128]{2,1,0:T(8,128)(2,1)}, bf16[4,256,128]...) while((s32[]{:T(128)}, f32[4,256,24,64]{1,3,2,0:T(8,128)}, ...), condition=%wide.region_4.5_spmd, body=%wide.region_3.4_spmd.sunk | while | flops 227606528 | bytes 3319905 | solution.py:127
  258.2 7.7 %copy.179 = f32[4,256,24,64]{1,0,3,2:T(4,128)} copy(f32[4,256,24,64]{1,3,2,0:T(8,128)S(1)} %fusion.74) | data formatting | bytes 12582912 | tf_op jit(solution)/shard_map/add | solution.py:161
  265.9 9.3 %reshape.314 = f32[2,512,1536]{1,0,2:T(2,128)} reshape(f32[4,256,24,64]{1,0,3,2:T(4,128)} %copy.179) | data formatting | bytes 12582912 | tf_op jit(solution)/shard_map/reshape | solution.py:162
  275.1 7.7 %multiply_reduce_fusion.5 = (f32[2,512]{1,0:T(2,128)S(1)}, f32[2,512,1536]{1,2,0:T(8,128)}) fusion(f32[2,512,3352]{1,2,0:T(8,128)} %get-tuple-element.316, f32[2,512,1536]{1,0,2:T(2,128)} %reshape.314), kind=kLoop, calls=%fused_computation.127 | loop fusion | flops 11009024 | bytes 18878464 | tf_op jit(solution)/shard_map/reduce_sum | solution.py:23
  282.8 10.6 %multiply_reduce_fusion.3 = (f32[1536]{0:T(1024)}, f32[2,512]{1,0:T(2,128)S(1)}, f32[2,512,1536]{1,2,0:T(8,128)}) fusion(f32[2,512,1536]{1,2,0:T(8,128)} %get-tuple-element.282, f32[2,512]{1,0:T(2,128)S(1)} %get-tuple-element.310, f32[1536]{0:T(1024)S(1)} %convert_element_type.172, bf16[1536,768]{1,0:T(8,128)(2,1)} %all-gather.6.cloned.1.call-done, ...), kind=kOutput, calls=%fused_computation.121 | convolution fusion | flops 2427713024 | bytes 16539648 | tf_op jit(solution)/shard_map/td,kd->tk/dot_general | solution.py:190
  293.5 8.8 %multiply_convert_fusion.16 = (bf16[2,512,1536]{1,2,0:T(8,128)(2,1)}, bf16[2,512,1536]{1,2,0:T(8,128)(2,1)S(1)}) fusion(f32[2,512,1536]{1,0,2:T(2,128)S(1)} %copy-done, f32[2,512,3352]{1,2,0:T(8,128)} %get-tuple-element.316, f32[2,512]{1,0:T(2,128)S(1)} %broadcast_multiply_fusion.4, f32[2,512,1536]{1,2,0:T(8,128)S(1)} %copy-done.2, ...), kind=kLoop, calls=%fused_computation.123 | loop fusion | flops 28311552 | bytes 31475712 | tf_op jit(solution)/shard_map/convert.2
  302.2 14.4 %copy.184 = bf16[2,512,1536]{1,0,2:T(2,128)(2,1)} copy(bf16[2,512,1536]{1,2,0:T(8,128)(2,1)S(1)} %get-tuple-element.294) | data formatting | bytes 6291456 | tf_op jit(solution)/shard_map/convert_element_type | solution.py:198
  316.7 8.6 %reshape.315 = bf16[4,256,24,64]{1,0,3,2:T(4,128)(2,1)} reshape(bf16[2,512,1536]{1,0,2:T(2,128)(2,1)} %copy.184) | data formatting | bytes 6291456 | tf_op jit(solution)/shard_map/reshape | solution.py:200
  325.2 8.2 %fusion.61 = f32[4,24,128,64]{2,3,1,0:T(8,128)S(1)} fusion(f32[4,24,256]{2,1,0:T(8,128)} %fusion.129, f32[4,256,128]{2,1,0:T(8,128)} %copy-done.23, bf16[4,256,24,64]{1,0,3,2:T(4,128)(2,1)} %reshape.315), kind=kOutput, calls=%fused_computation.92 | convolution fusion | flops 408944640 | bytes 6914048 | tf_op jit(solution)/shard_map/bhqn,bqhp->bhnp/dot_general | solution.py:205
  349.0 7.7 %convolution_bitcast_fusion.3 = f32[1536,768]{1,0:T(8,128)} fusion(bf16[2,512,768]{2,1,0:T(8,128)(2,1)S(1)} %copy-done.28, f32[2,512]{1,0:T(2,128)} %copy-done.68, f32[2,512,1536]{1,2,0:T(8,128)} %get-tuple-element.282, f32[1536]{0:T(1024)} %copy-done.52, f32[2,512]{1,0:T(2,128)} %copy-done.65), kind=kOutput, calls=%fused_computation.148 | convolution fusion | flops 2422996992 | bytes 12597248 | tf_op jit(solution)/shard_map/tk,td->kd/dot_general | solution.py:189
  371.4 61.5 %while.30 = (s32[]{:T(128)}, f32[4,256,24,64]{1,3,2,0:T(8,128)}, f32[4,256,128]{2,1,0:T(8,128)}, f32[4,256,128]{2,1,0:T(8,128)}, f32[4,24,256]{2,1,0:T(8,128)}, ...) while((s32[]{:T(128)}, f32[4,256,24,64]{1,3,2,0:T(8,128)}, ...), condition=%wide.region_12.13_spmd, body=%wide.region_7.12_spmd.sunk | while | flops 481284096 | bytes 6280337 | solution.py:202
  436.7 10.9 %fusion.52 = (f32[4,24,256]{2,1,0:T(8,128)}, bf16[4,24,256,128]{3,2,1,0:T(8,128)(2,1)S(1)}) fusion(f32[4,24,256]{2,1,0:T(8,128)S(1)} %copy-done.36, f32[4,256,128]{2,1,0:T(8,128)} %copy-done.23, bf16[4,24,128,64]{2,3,1,0:T(8,128)(2,1)} %bitcast.288, bf16[4,256,24,64]{1,0,3,2:T(4,128)(2,1)} %reshape.315), kind=kOutput, calls=%fused_computation.73 | convolution fusion | flops 415211520 | bytes 11730944 | tf_op jit(solution)/shard_map/bqhp,bhnp->bhqn/dot_general | solution.py:238
  483.5 7.5 copy.193
  491.0 9.4 %reshape.317 = f32[2,512,1536]{1,0,2:T(2,128)} reshape(f32[4,256,24,64]{1,0,3,2:T(4,128)} %copy.193) | data formatting | bytes 12582912 | tf_op jit(solution)/shard_map/reshape | solution.py:252
  511.0 10.0 %reduce-window.16 = f32[4,24,2,128]{3,1,2,0:T(8,128)S(1)} reduce-window(f32[4,24,2,128]{3,1,2,0:T(8,128)S(1)} %copy.206, f32[]{:T(128)} %constant.98.clone.1), window={size=1x1x1x128 pad=0_0x0_0x0_0x0_127}, to_apply=%region_15.16 | reduce-window | flops 3121152 | bytes 196612 | tf_op jit(solution)/shard_map/reduce-window.2
  527.3 19.6 %fusion.137 = (f32[1792]{0:T(1024)}, f32[1792]{0:T(1024)}, f32[1792]{0:T(1024)}, f32[1792]{0:T(1024)}, f32[1792]{0:T(1024)}, /*index=5*/f32[2,512,1792]{1,2,0:T(8,128)S(1)}) fusion(bf16[2,512,3352]{1,2,0:T(8,128)(2,1)} %get-tuple-element.315, bf16[2,512,1792]{1,2,0:T(8,128)(2,1)} %slice.154, bf16[2,3,1792]{1,2,0:T(8,128)(2,1)} %copy-done.8, ...), kind=kLoop, calls=%fused_computation.252 | loop fusion | flops 58711296 | bytes 29417472 | tf_op jit(solution)/shard_map/reduce_sum | solution.py:260
  546.9 9.2 %broadcast_multiply_fusion.3 = (f32[2,512,1792]{1,2,0:T(8,128)S(1)}, f32[2,512,1792]{1,2,0:T(8,128)}, f32[2,512,1792]{1,2,0:T(8,128)}, f32[2,512,1792]{1,2,0:T(8,128)}) fusion(f32[2,512,1792]{1,2,0:T(8,128)S(1)} %get-tuple-element.278, f32[1792]{0:T(1024)S(1)} %copy-done.40, f32[1792]{0:T(1024)} %copy-done.41, f32[1792]{0:T(1024)} %copy-done.42, ...), kind=kLoop, calls=%fused_computation.155 | loop fusion | flops 7340032 | bytes 36728832 | tf_op jit(solution)/shard_map/mul | solution.py:274
  556.0 11.4 %pad_add_fusion = f32[2,515,1792]{1,2,0:T(8,128)S(1)} fusion(f32[2,512,1792]{1,2,0:T(8,128)} %get-tuple-element.296, f32[2,512,1792]{1,2,0:T(8,128)} %get-tuple-element.297, f32[2,512,1792]{1,2,0:T(8,128)} %get-tuple-element.298, f32[2,512,1792]{1,2,0:T(8,128)S(1)} %get-tuple-element.295), kind=kLoop, calls=%fused_computation.81 | loop fusion | flops 5537280 | bytes 36743168 | tf_op jit(solution)/shard_map/add | solution.py:271
  576.3 17.5 %collective-permute-done.7 = bf16[2,3,1792]{2,0,1:T(2,128)(2,1)S(1)} collective-permute-done((bf16[2,3,1792]{2,0,1:T(2,128)(2,1)S(1)}, bf16[2,3,1792]{2,0,1:T(2,128)(2,1)S(1)}, u32[]{:S(2)}, u32[]{:S(2)}) %collective-permute-start.7) | collective-permute-done | bytes 21536 | tf_op jit(solution)/shard_map/ppermute | solution.py:19
  602.6 12.1 %convolution_bitcast_fusion.2 = f32[768,3352]{1,0:T(8,128)} fusion(bf16[2,512,24]{1,2,0:T(8,128)(2,1)S(1)} %get-tuple-element.277, bf16[2,512,1792]{1,2,0:T(8,128)(2,1)S(1)} %fusion.71, bf16[2,512,1536]{1,2,0:T(8,128)(2,1)} %get-tuple-element.293, bf16[2,512,768]{2,1,0:T(8,128)(2,1)S(1)} %copy-done.12, f32[768]{0:T(1024)S(1)} %copy-done.62, ...), kind=kOutput, calls=%fused_computation.94 | convolution fusion | flops 5295980544 | bytes 18742272 | tf_op jit(solution)/shard_map/td,te->de/dot_general | solution.py:290
  619.1 7.7 %fusion.94 = bf16[2,512,768]{2,1,0:T(8,128)(2,1)} fusion(bf16[2,512,768]{2,1,0:T(8,128)(2,1)S(1)} %copy-done.13, f32[2,512]{1,0:T(2,128)S(1)} %copy-done.69, bf16[1536,768]{1,0:T(8,128)(2,1)S(1)} %copy-done.75, f32[2,512,1536]{1,2,0:T(8,128)} %get-tuple-element.282, f32[1536]{0:T(1024)S(1)} %copy-done.53, f32[2,512]{1,0:T(2,128)S(1)} %copy-done.66), kind=kOutput, calls=%fused_computation.161 | convolution fusion | flops 2423783424 | bytes 11810816 | tf_op jit(solution)/shard_map/dot_general | solution.py:171
  627.0 11.0 %fusion.99 = (f32[768]{0:T(1024)S(1)}, f32[2,512]{1,0:T(2,128)S(1)}, f32[2,512,768]{2,1,0:T(8,128)}) fusion(bf16[2,512,768]{2,1,0:T(8,128)(2,1)S(1)} %copy-done.13, f32[2,512]{1,0:T(2,128)S(1)} %copy-done.60, f32[768]{0:T(1024)S(1)} %copy-done.62, bf16[768,3352]{1,0:T(8,128)(2,1)} %all-gather.4.cloned.1.call-done, ...), kind=kOutput, calls=%fused_computation.166 | convolution fusion | flops 5298337792 | bytes 16746496 | tf_op jit(solution)/shard_map/te,de->td/dot_general | solution.py:291
  638.1 38.9 %all-reduce.13 = (f32[768]{0:T(1024)S(1)}, f32[4,1792]{1,0:T(4,128)S(1)}, f32[1792]{0:T(1024)S(1)}, f32[24]{0:T(128)}, f32[24]{0:T(128)}, /*index=5*/f32[24]{0:T(128)}, f32[1536]{0:T(1024)S(1)}) all-reduce(f32[768]{0:T(1024)S(1)} %get-tuple-element.222, ...), channel_id=2, replica_groups=mesh['dp'=8,'seq'=4] {'dp','seq'}, use_global_device_ids=true, to_apply=%region_19.20.clone | all-reduce | flops 11336 | bytes 90688
  682.7 72.5 %reduce-scatter.8.cloned.1.call-done = f32[24,3352]{1,0:T(8,128)} async-done(((f32[768,3352]{1,0:T(8,128)}), f32[24,3352]{1,0:T(8,128)}) %reduce-scatter.8.cloned.1.call-update) | async-done | bytes 321808
  (360 shorter events, 263.0 us)
Async XLA Ops:
  7.2 91.2 %all-gather.4.cloned.1.call-start = ((), (), s32[]{:S(2)}) async-start(), calls=%async_computation.2 | async-start | bytes 5474304 | tf_op jit(solution)/shard_map/all_gather | solution.py:88
  8.9 273.9 %all-gather.6.cloned.1.call-start = ((), (), s32[]{:S(2)}) async-start(), calls=%async_computation.3 | async-start | bytes 2433024 | tf_op jit(solution)/shard_map/all_gather | solution.py:92
  9.6 103.8 %copy-start.72 = (f32[24]{0:T(128)}, f32[24]{0:T(128)S(1)}, u32[]{:S(2)}) copy-start(f32[24]{0:T(128)S(1)} %exp.45) | copy-start | bytes 292
  54.5 56.7 %copy-start.61 = (f32[768]{0:T(1024)}, f32[768]{0:T(1024)S(1)}, u32[]{:S(2)}) copy-start(f32[768]{0:T(1024)S(1)} %convert_element_type.157) | copy-start | bytes 9220
  96.0 31.3 %copy-start.39 = (f32[1792]{0:T(1024)}, f32[1792]{0:T(1024)S(1)}, u32[]{:S(2)}) copy-start(f32[1792]{0:T(1024)S(1)} %get-tuple-element.224) | copy-start | bytes 21508
  96.0 31.3 %copy-start.41 = (f32[1792]{0:T(1024)}, f32[1792]{0:T(1024)S(1)}, u32[]{:S(2)}) copy-start(f32[1792]{0:T(1024)S(1)} %get-tuple-element.225) | copy-start | bytes 21508
  96.0 31.3 %copy-start.42 = (f32[1792]{0:T(1024)}, f32[1792]{0:T(1024)S(1)}, u32[]{:S(2)}) copy-start(f32[1792]{0:T(1024)S(1)} %get-tuple-element.226) | copy-start | bytes 21508
  96.0 31.3 %copy-start.43 = (f32[1792]{0:T(1024)}, f32[1792]{0:T(1024)S(1)}, u32[]{:S(2)}) copy-start(f32[1792]{0:T(1024)S(1)} %get-tuple-element.227) | copy-start | bytes 21508
  116.3 79.6 %copy-start.44 = (f32[4,24,2]{1,2,0:T(2,128)}, f32[4,24,2]{1,2,0:T(2,128)S(1)}, u32[]{:S(2)}) copy-start(f32[4,24,2]{1,2,0:T(2,128)S(1)} %copy.167) | copy-start | bytes 2308
  116.7 52.7 %copy-start.63 = (f32[2,1,24]{2,1,0:T(1,128)}, f32[2,1,24]{2,1,0:T(1,128)S(1)}, u32[]{:S(2)}) copy-start(f32[2,1,24]{2,1,0:T(1,128)S(1)} %get-tuple-element.311) | copy-start | bytes 580
  116.9 22.9 %copy-start.16 = (f32[4,24,256]{1,0,2:T(4,128)}, f32[4,24,256]{1,0,2:T(4,128)S(1)}, u32[]{:S(2)}) copy-start(f32[4,24,256]{1,0,2:T(4,128)S(1)} %bitcast_multiply_fusion.4) | copy-start | bytes 294916
  119.1 7.7 %collective-permute-start = (bf16[2,3,1792]{2,0,1:T(2,128)(2,1)S(1)}, bf16[2,3,1792]{2,0,1:T(2,128)(2,1)S(1)}, u32[]{:S(2)}, u32[]{:S(2)}) collective-permute-start(bf16[2,3,1792]{2,0,1:T(2,128)(2,1)S(1)} %copy.158), channel_id=1, source_target_pairs={{0,1},{1,2},{2,3},{4,5},{5,6},{6,7},{8,9},{9,10},{10,11},{12,13},{... | collective-permute-start | bytes 64520 | tf_op jit(solution)/shard_map/ppermute | solution.py:19
  121.9 218.2 %copy-start.54 = (f32[2,24]{1,0:T(2,128)}, f32[2,24]{1,0:T(2,128)S(1)}, u32[]{:S(2)}) copy-start(f32[2,24]{1,0:T(2,128)S(1)} %get-tuple-element.286) | copy-start | bytes 580
  169.3 24.1 %copy-start.37 = (f32[48,768]{1,0:T(8,128)S(1)}, f32[48,768]{1,0:T(8,128)}, u32[]{:S(2)}) copy-start(f32[48,768]{1,0:T(8,128)} %param.28) | copy-start | bytes 442372
  169.4 24.8 %copy-start.74 = (s32[2]{0:T(128)S(1)}, s32[2]{0:T(128)}, u32[]{:S(2)}) copy-start(s32[2]{0:T(128)} %param.19) | copy-start | bytes 28
  169.8 4.9 collective-permute-start.1
  176.1 24.5 %collective-permute-start.2 = (f32[2,24,128,64]{2,3,1,0:T(8,128)}, f32[2,24,128,64]{2,3,1,0:T(8,128)}, u32[]{:S(2)}, u32[]{:S(2)}) collective-permute-start(f32[2,24,128,64]{2,3,1,0:T(8,128)} %multiply_add_fusion.3), channel_id=1, source_target_pairs={{0,1},{1,2},{2,3},{4,5},{5,6},{6,7},{8,9},{9,10},{10,11},{12,13},{... | collective-permute-start | bytes 4718600 | tf_op jit(solution)/shard_map/ppermute | solution.py:19
  194.1 488.6 %reduce-scatter.6.cloned.1.call-start = ((), (), s32[]{:S(2)}) async-start(), calls=%async_computation.4 | async-start | bytes 4866048 | tf_op jit(solution)/shard_map/reduce_scatter | solution.py:306
  194.2 99.3 %copy-start.52 = (f32[1536]{0:T(1024)}, f32[1536]{0:T(1024)S(1)}, u32[]{:S(2)}) copy-start(f32[1536]{0:T(1024)S(1)} %convert_element_type.172) | copy-start | bytes 18436
  194.3 88.5 %copy-start.68 = (f32[2,512]{1,0:T(2,128)}, f32[2,512]{1,0:T(2,128)S(1)}, u32[]{:S(2)}) copy-start(f32[2,512]{1,0:T(2,128)S(1)} %compare_convert_fusion) | copy-start | bytes 12292
  203.8 45.1 %collective-permute-start.3 = (f32[2,24,128,64]{2,3,1,0:T(8,128)}, f32[2,24,128,64]{2,3,1,0:T(8,128)}, u32[]{:S(2)}, u32[]{:S(2)}) collective-permute-start(f32[2,24,128,64]{2,3,1,0:T(8,128)} %multiply_add_fusion.2), channel_id=1, source_target_pairs={{0,1},{1,2},{2,3},{4,5},{5,6},{6,7},{8,9},{9,10},{10,11},{12,13},{... | collective-permute-start | bytes 4718600 | tf_op jit(solution)/shard_map/ppermute | solution.py:19
  333.9 6.2 collective-permute-start.4
  341.4 22.1 %collective-permute-start.5 = (f32[2,24,128,64]{2,3,1,0:T(8,128)}, f32[2,24,128,64]{2,3,1,0:T(8,128)}, u32[]{:S(2)}, u32[]{:S(2)}) collective-permute-start(f32[2,24,128,64]{2,3,1,0:T(8,128)} %multiply_add_fusion.1), channel_id=1, source_target_pairs={{1,0},{2,1},{3,2},{5,4},{6,5},{7,6},{9,8},{10,9},{11,10},{13,12},{... | collective-permute-start | bytes 4718600 | tf_op jit(solution)/shard_map/ppermute | solution.py:19
  356.8 398.4 %reduce-scatter.8.cloned.1.call-start = ((), (), s32[]{:S(2)}) async-start(), calls=%async_computation.5 | async-start | bytes 10948608
  366.8 88.7 %collective-permute-start.6 = (f32[2,24,128,64]{2,3,1,0:T(8,128)}, f32[2,24,128,64]{2,3,1,0:T(8,128)}, u32[]{:S(2)}, u32[]{:S(2)}) collective-permute-start(f32[2,24,128,64]{2,3,1,0:T(8,128)} %multiply_add_fusion), channel_id=1, source_target_pairs={{1,0},{2,1},{3,2},{5,4},{6,5},{7,6},{9,8},{10,9},{11,10},{13,12},{... | collective-permute-start | bytes 4718600 | tf_op jit(solution)/shard_map/ppermute | solution.py:19
  371.4 65.3 %copy-start.36 = (f32[4,24,256]{2,1,0:T(8,128)S(1)}, f32[4,24,256]{2,1,0:T(8,128)}, u32[]{:S(2)}) copy-start(f32[4,24,256]{2,1,0:T(8,128)} %fusion.129) | copy-start | bytes 294916
  573.6 20.2 %collective-permute-start.7 = (bf16[2,3,1792]{2,0,1:T(2,128)(2,1)S(1)}, bf16[2,3,1792]{2,0,1:T(2,128)(2,1)S(1)}, u32[]{:S(2)}, u32[]{:S(2)}) collective-permute-start(bf16[2,3,1792]{2,0,1:T(2,128)(2,1)S(1)} %copy.199), channel_id=1, source_target_pairs={{1,0},{2,1},{3,2},{5,4},{6,5},{7,6},{9,8},{10,9},{11,10},{13,12},{... | collective-permute-start | bytes 64520 | tf_op jit(solution)/shard_map/ppermute | solution.py:19
  576.3 26.4 %copy-start.60 = (f32[2,512]{1,0:T(2,128)S(1)}, f32[2,512]{1,0:T(2,128)}, u32[]{:S(2)}) copy-start(f32[2,512]{1,0:T(2,128)} %copy-done.59) | copy-start | bytes 12292
  576.3 26.4 %copy-start.62 = (f32[768]{0:T(1024)S(1)}, f32[768]{0:T(1024)}, u32[]{:S(2)}) copy-start(f32[768]{0:T(1024)} %copy-done.61) | copy-start | bytes 9220
  627.0 52.3 %copy-start.14 = (bf16[2,512,768]{2,1,0:T(8,128)(2,1)S(1)}, bf16[2,512,768]{2,1,0:T(8,128)(2,1)}, u32[]{:S(2)}) copy-start(bf16[2,512,768]{2,1,0:T(8,128)(2,1)} %param.18) | copy-start | bytes 4718596
  627.0 52.3 %copy-start.29 = (bf16[2,512,768]{2,1,0:T(8,128)(2,1)S(1)}, bf16[2,512,768]{2,1,0:T(8,128)(2,1)}, u32[]{:S(2)}) copy-start(bf16[2,512,768]{2,1,0:T(8,128)(2,1)} %param.29) | copy-start | bytes 4718596
  627.0 52.3 %copy-start.58 = (f32[2,512]{1,0:T(2,128)S(1)}, f32[2,512]{1,0:T(2,128)}, u32[]{:S(2)}) copy-start(f32[2,512]{1,0:T(2,128)} %get-tuple-element.307) | copy-start | bytes 12292
  (59 other events, 458.7 us)
Sparse Core Ops, SparseCore 0:
  11.5 68.4 all-gather.3
  194.2 55.1 all-gather.5
  356.9 123.3 reduce-scatter.5
  614.9 140.2 reduce-scatter.7
where the time goes:
time: 772 us; the launch traced here: 762 us
  matrix products  187 us (24%)
  local copies, waits for them, and re-layouts  151 us (20%)
  other arithmetic  139 us (18%)
  blocking collectives  122 us (16%)
  waiting for transfers between devices  105 us (14%)
  starting transfers between devices  43.2 us (6%)
  between operations  15.5 us (2%)
    unnamed x2, blocking collectives  81.2 us
    unnamed x5, waiting for transfers between devices  72.5 us
    ppermute x8, starting transfers between devices, from_behind(): return lax.ppermute(block, axis, route)  43 us
    all_gather x1, blocking collectives, per_device(): lax.all_gather(shards[2], ('dp', 'seq'), axis=1, tiled=True)  40.5 us
    another operation x12, other arithmetic  39.2 us
    ppermute x8, waiting for transfers between devices, from_behind(): return lax.ppermute(block, axis, route)  32 us
    dot_general x4, matrix products, intra_backward(): jnp.einsum('qhp,rhp->hqr', grad_group, x_group, preferred_element_type=jn...  22 us
    reduce_sum x1, other arithmetic, per_device(): grad_conv_bias = jnp.sum(grad_pre, axis=(0, 1))  19.6 us
  transfers between devices with their start and end apart: 12, of which 5 were waited for; matrix products, arithmetic and copies ran while one was open for 46% of the time, Pallas kernels for 0%

commit v1 on v0

--- a/solution.py
+++ b/solution.py
@@ -11,6 +11,35 @@
 DI = 1536
 CD = 1792
 epsilon = 1e-05
+
+
+def drive_the_rails(load, out_dim):
+    load = jnp.moveaxis(load, 0, out_dim)
+    clean = load.shape
+    return load.reshape(
+        *clean[:out_dim], clean[out_dim] * clean[out_dim + 1], *clean[out_dim + 2 :]
+    )
+
+
+def form_islands(arr_in, device_axis):
+    earlier = arr_in[None]
+    cores_n = lax.axis_size(device_axis)
+    for src_i in range(cores_n.bit_length() - 1):
+        part_next = 1 << src_i
+        kept_rows = []
+        k0 = 0
+        while k0 < cores_n:
+            kept_rows.append((k0, k0 ^ part_next))
+            k0 += 1
+        back = lax.ppermute(earlier, device_axis, perm=kept_rows)
+        main = jnp.stack([earlier, back])
+        b_next = lax.axis_index(device_axis) >> src_i & 1
+        earlier = jnp.where(b_next == 0, main, main[::-1]).reshape(-1, *arr_in.shape)
+    return earlier
+
+
+def load_paths(u_in, sample, in_dim):
+    return drive_the_rails(form_islands(u_in, sample), in_dim)
 
 
 def from_behind(block, axis, distance):
@@ -86,7 +115,7 @@
     gathered = (
         lax.all_gather(shards[0], ("dp", "seq"), axis=0, tiled=True),
         lax.all_gather(shards[1], ("dp", "seq"), axis=0, tiled=True),
-        lax.all_gather(shards[2], ("dp", "seq"), axis=1, tiled=True),
+        load_paths(shards[2], sample=("dp", "seq"), in_dim=1),
         lax.all_gather(shards[3], ("dp", "seq"), axis=0, tiled=True),
         lax.all_gather(shards[4], ("dp", "seq"), axis=0, tiled=True),
         lax.all_gather(shards[5], ("dp", "seq"), axis=0, tiled=True),

time: 772 us -> 811 us (1.051)
  blocking collectives: 122 us -> 147 us
  starting transfers between devices: 43.2 us -> 55.1 us
  waiting for transfers between devices: 105 us -> 94 us
    all_gather x1, blocking collectives: 40.5 us -> 65.7 us  [per_device(): lax.all_gather(back_shards[2], ('dp', 'seq'), axis=1, tiled=True)]
    ppermute x8, waiting for transfers between devices: 32 us -> 8.63 us  [from_behind(): return lax.ppermute(block, axis, route)]
    ppermute x0 -> x5, starting transfers between devices: none -> 10.5 us  [form_islands(): back = lax.ppermute(earlier, device_axis, perm=kept_rows)]
    all_gather x1, waiting for transfers between devices: 0.01 us -> 8.77 us  [per_device(): lax.all_gather(shards[1], ('dp', 'seq'), axis=0, tiled=True)]
    another operation x12 -> x18, other arithmetic: 39.2 us -> 39.3 us
  transfers between devices with their start and end apart: 12 -> 17, of which waited for: 5 -> 8; matrix products, arithmetic and copies ran while one was open for 46% -> 45% of each run, Pallas kernels for 0% -> 0%
where the time goes in v1:
time: 811 us; the launch traced here: 800 us
  matrix products  190 us (23%)
  local copies, waits for them, and re-layouts  158 us (19%)
  blocking collectives  147 us (18%)
  other arithmetic  141 us (17%)
  waiting for transfers between devices  94 us (12%)
  starting transfers between devices  55.1 us (7%)
  between operations  15.5 us (2%)
    unnamed x2, blocking collectives  81.1 us
    unnamed x5, waiting for transfers between devices  72.6 us
    all_gather x1, blocking collectives, per_device(): lax.all_gather(back_shards[2], ('dp', 'seq'), axis=1, tiled=True)  65.7 us
    ppermute x8, starting transfers between devices, from_behind(): return lax.ppermute(block, axis, route)  44.5 us
    another operation x12, other arithmetic  39.2 us
    dot_general x4, matrix products, intra_backward(): jnp.einsum('qhp,rhp->hqr', grad_group, x_group, preferred_element_type=jn...  22 us
    reduce_sum x1, other arithmetic, per_device(): grad_conv_bias = jnp.sum(grad_pre, axis=(0, 1))  19.2 us
    dot_general x4, matrix products, intra_forward(): jnp.einsum('hqr,rhp->qhp', mixing, x_group, preferred_element_type=jnp.fl...  17.6 us
  transfers between devices with their start and end apart: 17, of which 8 were waited for; matrix products, arithmetic and copies ran while one was open for 45% of the time, Pallas kernels for 0%

profile of v1, /device:TPU:0, one launch (start us, length us, event | category | flops | bytes accessed | tf_op | source)
XLA Modules:
  0.0 799.7 jit_solution(4673710329352124289)
XLA Ops:
  29.9 41.2 %all-reduce.14 = (bf16[768]{0:T(1024)(128)(2,1)S(1)}, bf16[1792]{0:T(1024)(128)(2,1)S(1)}, bf16[1536]{0:T(1024)(128)(2,1)S(1)}) all-reduce(bf16[768]{0:T(1024)(128)(2,1)S(1)} %dynamic-update-slice.4, bf16[1792]{0:T(1024)(128)(2,1)S(1)} %dynamic-update-slice.3, ...), channel_id=1, replica_groups=mesh['dp'=8,'seq'=4] {'dp','seq'}, use_global_device_ids=true, to_apply=%add.6 | all-reduce | flops 4096 | bytes 16384
  71.8 8.8 %all-gather.4.cloned.1.call-done = bf16[768,3352]{1,0:T(8,128)(2,1)} async-done(((bf16[24,3352]{1,0:T(8,128)(2,1)}), bf16[768,3352]{1,0:T(8,128)(2,1)}) %all-gather.4.cloned.1.call-update) | async-done | bytes 5148688 | tf_op jit(solution)/shard_map/all_gather | solution.py:117
  80.6 15.2 %fusion.147 = (bf16[2,512,3352]{1,2,0:T(8,128)(2,1)}, f32[2,512,3352]{1,2,0:T(8,128)S(1)}) fusion(bf16[768,3352]{1,0:T(8,128)(2,1)} %all-gather.4.cloned.1.call-done, bf16[2,512,768]{2,1,0:T(8,128)(2,1)} %param.18, f32[768]{0:T(1024)S(1)} %convert_element_type.168, f32[2,512]{1,0:T(2,128)S(1)} %get-tuple-element.312), kind=kOutput, calls=%fused_computation.275 | convolution fusion | flops 5278818304 | bytes 27323392 | tf_op jit(solution)/shard_map/dot_general | solution.py:133
  115.8 12.4 %multiply_convert_fusion.14 = (bf16[2,512,1792]{1,2,0:T(8,128)(2,1)S(1)}, f32[2,512,1792]{1,2,0:T(8,128)}) fusion(bf16[2,512,1792]{1,2,0:T(8,128)(2,1)} %slice.170, f32[1792]{0:T(1024)S(1)} %mul.546, bf16[2,3,1792]{1,2,0:T(8,128)(2,1)S(1)} %copy.158, f32[1792]{0:T(1024)S(1)} %mul.543, f32[1792]{0:T(1024)S(1)} %mul.540, f32[1792]{0:T(1024)S(1)} %mul.532, ...), kind=kLoop, calls=%fused_computation.107 | loop fusion | flops 47710208 | bytes 14737408 | tf_op jit(solution)/shard_map/convert.10
  129.3 14.5 %copy.159 = bf16[2,512,1536]{1,0,2:T(2,128)(2,1)} copy(bf16[2,512,1536]{1,2,0:T(8,128)(2,1)S(1)} %slice.178) | data formatting | bytes 6291456 | tf_op jit(solution)/shard_map/slice | solution.py:149
  143.8 7.4 reshape.340
  165.8 17.7 %collective-permute-start.7 = (f32[2,24,128,64]{2,3,1,0:T(8,128)}, f32[2,24,128,64]{2,3,1,0:T(8,128)}, u32[]{:S(2)}, u32[]{:S(2)}) collective-permute-start(f32[2,24,128,64]{2,3,1,0:T(8,128)} %multiply_add_fusion.3), channel_id=1, source_target_pairs={{0,1},{1,2},{2,3},{4,5},{5,6},{6,7},{8,9},{9,10},{10,11},{12,13},{... | collective-permute-start | bytes 4718600 | tf_op jit(solution)/shard_map/ppermute | solution.py:48
  194.0 15.5 %collective-permute-start.8 = (f32[2,24,128,64]{2,3,1,0:T(8,128)}, f32[2,24,128,64]{2,3,1,0:T(8,128)}, u32[]{:S(2)}, u32[]{:S(2)}) collective-permute-start(f32[2,24,128,64]{2,3,1,0:T(8,128)} %multiply_add_fusion.2), channel_id=1, source_target_pairs={{0,1},{1,2},{2,3},{4,5},{5,6},{6,7},{8,9},{9,10},{10,11},{12,13},{... | collective-permute-start | bytes 4718600 | tf_op jit(solution)/shard_map/ppermute | solution.py:48
  212.9 24.9 %while.29 = (s32[]{:T(128)}, f32[4,256,24,64]{1,3,2,0:T(8,128)}, bf16[4,256,24,64]{1,3,2,0:T(8,128)(2,1)}, bf16[4,256,128]{2,1,0:T(8,128)(2,1)}, bf16[4,256,128]...) while((s32[]{:T(128)}, f32[4,256,24,64]{1,3,2,0:T(8,128)}, ...), condition=%wide.region_4.5_spmd, body=%wide.region_3.4_spmd.sunk | while | flops 227606528 | bytes 3319905 | solution.py:156
  248.2 7.6 copy.178
  255.8 9.3 %reshape.347 = f32[2,512,1536]{1,0,2:T(2,128)} reshape(f32[4,256,24,64]{1,0,3,2:T(4,128)} %copy.178) | data formatting | bytes 12582912 | tf_op jit(solution)/shard_map/reshape | solution.py:191
  265.0 7.6 multiply_reduce_fusion.5
  272.8 10.6 %multiply_reduce_fusion.3 = (f32[1536]{0:T(1024)}, f32[2,512]{1,0:T(2,128)S(1)}, f32[2,512,1536]{1,2,0:T(8,128)}) fusion(f32[2,512,1536]{1,2,0:T(8,128)} %get-tuple-element.286, f32[2,512]{1,0:T(2,128)S(1)} %get-tuple-element.314, f32[1536]{0:T(1024)S(1)} %convert_element_type.183, bf16[1536,768]{1,0:T(8,128)(2,1)} %all-gather.6.cloned.1.call-done, ...), kind=kOutput, calls=%fused_computation.121 | convolution fusion | flops 2427713024 | bytes 16539648 | tf_op jit(solution)/shard_map/td,kd->tk/dot_general | solution.py:219
  283.4 8.8 %multiply_convert_fusion.16 = (bf16[2,512,1536]{1,2,0:T(8,128)(2,1)}, bf16[2,512,1536]{1,2,0:T(8,128)(2,1)S(1)}) fusion(f32[2,512,1536]{1,0,2:T(2,128)S(1)} %copy-done, f32[2,512,3352]{1,2,0:T(8,128)} %copy-done.7, f32[2,512]{1,0:T(2,128)S(1)} %broadcast_multiply_fusion.4, f32[2,512,1536]{1,2,0:T(8,128)S(1)} %copy-done.2, ...), kind=kLoop, calls=%fused_computation.123 | loop fusion | flops 28311552 | bytes 31475712 | tf_op jit(solution)/shard_map/convert.4
  292.1 14.4 %copy.184 = bf16[2,512,1536]{1,0,2:T(2,128)(2,1)} copy(bf16[2,512,1536]{1,2,0:T(8,128)(2,1)S(1)} %get-tuple-element.298) | data formatting | bytes 6291456 | tf_op jit(solution)/shard_map/convert_element_type | solution.py:227
  306.6 8.6 %reshape.348 = bf16[4,256,24,64]{1,0,3,2:T(4,128)(2,1)} reshape(bf16[2,512,1536]{1,0,2:T(2,128)(2,1)} %copy.184) | data formatting | bytes 6291456 | tf_op jit(solution)/shard_map/reshape | solution.py:229
  315.1 8.2 %fusion.61 = f32[4,24,128,64]{2,3,1,0:T(8,128)S(1)} fusion(f32[4,24,256]{2,1,0:T(8,128)} %fusion.131, f32[4,256,128]{2,1,0:T(8,128)} %copy-done.24, bf16[4,256,24,64]{1,0,3,2:T(4,128)(2,1)} %reshape.348), kind=kOutput, calls=%fused_computation.92 | convolution fusion | flops 408944640 | bytes 6914048 | tf_op jit(solution)/shard_map/bhqn,bqhp->bhnp/dot_general | solution.py:234
  332.5 65.7 %all-gather = bf16[32,56,4]{1,2,0:T(4,128)(2,1)S(1)} all-gather(bf16[1,56,4]{1,2,0:T(4,128)(2,1)S(1)} %get-tuple-element.315), channel_id=1, replica_groups=mesh['dp'=8,'seq'=4] {'dp','seq'}, dimensions={0}, use_global_device_ids=true | all-gather | bytes 14784 | tf_op jit(solution)/shard_map/all_gather | solution.py:208
  406.7 7.8 convolution_bitcast_fusion.3
  422.6 61.4 %while.30 = (s32[]{:T(128)}, f32[4,256,24,64]{1,3,2,0:T(8,128)}, f32[4,256,128]{2,1,0:T(8,128)}, f32[4,256,128]{2,1,0:T(8,128)}, f32[4,24,256]{2,1,0:T(8,128)}, ...) while((s32[]{:T(128)}, f32[4,256,24,64]{1,3,2,0:T(8,128)}, ...), condition=%wide.region_12.13_spmd, body=%wide.region_7.12_spmd.sunk | while | flops 481284096 | bytes 6280337 | solution.py:231
  487.8 11.1 %fusion.52 = (f32[4,24,256]{2,1,0:T(8,128)}, bf16[4,24,256,128]{3,2,1,0:T(8,128)(2,1)S(1)}) fusion(f32[4,24,256]{2,1,0:T(8,128)S(1)} %copy-done.37, f32[4,256,128]{2,1,0:T(8,128)} %copy-done.24, bf16[4,24,128,64]{2,3,1,0:T(8,128)(2,1)} %bitcast.312, bf16[4,256,24,64]{1,0,3,2:T(4,128)(2,1)} %reshape.348), kind=kOutput, calls=%fused_computation.73 | convolution fusion | flops 415211520 | bytes 11730944 | tf_op jit(solution)/shard_map/bqhp,bhnp->bhqn/dot_general | solution.py:267
  534.6 7.6 copy.193
  542.2 9.4 %reshape.350 = f32[2,512,1536]{1,0,2:T(2,128)} reshape(f32[4,256,24,64]{1,0,3,2:T(4,128)} %copy.193) | data formatting | bytes 12582912 | tf_op jit(solution)/shard_map/reshape | solution.py:281
  562.3 10.0 %reduce-window.16 = f32[4,24,2,128]{3,1,2,0:T(8,128)S(1)} reduce-window(f32[4,24,2,128]{3,1,2,0:T(8,128)S(1)} %copy.206, f32[]{:T(128)} %constant.105.clone.1), window={size=1x1x1x128 pad=0_0x0_0x0_0x0_127}, to_apply=%region_15.16 | reduce-window | flops 3121152 | bytes 196612 | tf_op jit(solution)/shard_map/reduce-window.2
  578.0 19.2 %fusion.139 = (f32[1792]{0:T(1024)S(1)}, f32[1792]{0:T(1024)S(1)}, f32[1792]{0:T(1024)S(1)}, f32[1792]{0:T(1024)S(1)}, f32[1792]{0:T(1024)S(1)}, /*index=5*/f32[2,512,1792]{1,2,0:T(8,128)S(1)}) fusion(bf16[2,512,3352]{1,2,0:T(8,128)(2,1)} %get-tuple-element.324, bf16[2,512,1792]{1,2,0:T(8,128)(2,1)} %slice.170, bf16[2,3,1792]{1,2,0:T(8,128)(2,1)} %copy-done.9, ...), kind=kLoop, calls=%fused_computation.271 | loop fusion | flops 58711296 | bytes 29417472 | tf_op jit(solution)/shard_map/reduce_sum | solution.py:289
  597.2 10.6 %broadcast_multiply_fusion.3 = (f32[2,512,1792]{1,2,0:T(8,128)}, f32[2,512,1792]{1,2,0:T(8,128)}, f32[2,512,1792]{1,2,0:T(8,128)}, f32[2,512,1792]{1,2,0:T(8,128)}) fusion(f32[2,512,1792]{1,2,0:T(8,128)S(1)} %get-tuple-element.282, f32[1792]{0:T(1024)S(1)} %copy-done.43, f32[1792]{0:T(1024)S(1)} %copy-done.44, f32[1792]{0:T(1024)S(1)} %copy-done.45, ...), kind=kLoop, calls=%fused_computation.155 | loop fusion | flops 7340032 | bytes 36728832 | tf_op jit(solution)/shard_map/mul | solution.py:303
  607.9 12.7 %pad_add_fusion = f32[2,515,1792]{1,2,0:T(8,128)S(1)} fusion(f32[2,512,1792]{1,2,0:T(8,128)} %get-tuple-element.300, f32[2,512,1792]{1,2,0:T(8,128)} %get-tuple-element.301, f32[2,512,1792]{1,2,0:T(8,128)} %get-tuple-element.302, f32[2,512,1792]{1,2,0:T(8,128)} %get-tuple-element.299), kind=kLoop, calls=%fused_computation.81 | loop fusion | flops 5537280 | bytes 36743168 | tf_op jit(solution)/shard_map/add | solution.py:300
  639.1 12.2 %convolution_bitcast_fusion.2 = f32[768,3352]{1,0:T(8,128)} fusion(bf16[2,512,24]{1,2,0:T(8,128)(2,1)S(1)} %get-tuple-element.281, bf16[2,512,1792]{1,2,0:T(8,128)(2,1)S(1)} %fusion.71, bf16[2,512,1536]{1,2,0:T(8,128)(2,1)} %get-tuple-element.297, bf16[2,512,768]{2,1,0:T(8,128)(2,1)S(1)} %copy-done.13, f32[768]{0:T(1024)S(1)} %copy-done.57, ...), kind=kOutput, calls=%fused_computation.94 | convolution fusion | flops 5295980544 | bytes 18742272 | tf_op jit(solution)/shard_map/td,te->de/dot_general | solution.py:319
  655.7 7.6 fusion.94
  663.5 11.1 %fusion.99 = (f32[768]{0:T(1024)S(1)}, f32[2,512]{1,0:T(2,128)S(1)}, f32[2,512,768]{2,1,0:T(8,128)}) fusion(bf16[2,512,768]{2,1,0:T(8,128)(2,1)S(1)} %copy-done.14, f32[2,512]{1,0:T(2,128)S(1)} %copy-done.55, f32[768]{0:T(1024)S(1)} %copy-done.57, bf16[768,3352]{1,0:T(8,128)(2,1)} %all-gather.4.cloned.1.call-done, ...), kind=kOutput, calls=%fused_computation.166 | convolution fusion | flops 5298337792 | bytes 16746496 | tf_op jit(solution)/shard_map/te,de->td/dot_general | solution.py:320
  674.6 39.9 %all-reduce.13 = (f32[768]{0:T(1024)S(1)}, f32[4,1792]{1,0:T(4,128)S(1)}, f32[1792]{0:T(1024)S(1)}, f32[24]{0:T(128)}, f32[24]{0:T(128)}, /*index=5*/f32[24]{0:T(128)}, f32[1536]{0:T(1024)S(1)}) all-reduce(f32[768]{0:T(1024)S(1)} %get-tuple-element.222, ...), channel_id=2, replica_groups=mesh['dp'=8,'seq'=4] {'dp','seq'}, use_global_device_ids=true, to_apply=%region_19.20.clone | all-reduce | flops 11336 | bytes 90688
  720.2 72.5 %reduce-scatter.8.cloned.1.call-done = f32[24,3352]{1,0:T(8,128)} async-done(((f32[768,3352]{1,0:T(8,128)}), f32[24,3352]{1,0:T(8,128)}) %reduce-scatter.8.cloned.1.call-update) | async-done | bytes 321808
  (376 shorter events, 278.9 us)
Async XLA Ops:
  7.2 73.4 %all-gather.4.cloned.1.call-start = ((), (), s32[]{:S(2)}) async-start(), calls=%async_computation.2 | async-start | bytes 5474304 | tf_op jit(solution)/shard_map/all_gather | solution.py:117
  8.9 263.8 %all-gather.6.cloned.1.call-start = ((), (), s32[]{:S(2)}) async-start(), calls=%async_computation.3 | async-start | bytes 2433024 | tf_op jit(solution)/shard_map/all_gather | solution.py:121
  9.6 1.3 collective-permute-start
  10.9 4.4 collective-permute-start.1
  15.4 3.7 collective-permute-start.2
  19.1 4.0 collective-permute-start.3
  23.2 48.0 %collective-permute-start.4 = (bf16[16,4,56]{2,1,0:T(4,128)(2,1)S(1)}, bf16[16,4,56]{2,1,0:T(4,128)(2,1)S(1)}, u32[]{:S(2)}, u32[]{:S(2)}) collective-permute-start(bf16[16,4,56]{2,1,0:T(4,128)(2,1)S(1)} %bitcast.323), channel_id=1, source_target_pairs={{0,16},{1,17},{2,18},{3,19},{4,20},{5,21},{6,22},{7,23},{8,24},{9,... | collective-permute-start | bytes 21512 | tf_op jit(solution)/shard_map/ppermute | solution.py:34
  26.6 69.1 %copy-start.54 = (f32[2,512]{1,0:T(2,128)}, f32[2,512]{1,0:T(2,128)S(1)}, u32[]{:S(2)}) copy-start(f32[2,512]{1,0:T(2,128)S(1)} %get-tuple-element.312) | copy-start | bytes 12292
  27.3 74.6 %copy-start.67 = (f32[24]{0:T(128)}, f32[24]{0:T(128)S(1)}, u32[]{:S(2)}) copy-start(f32[24]{0:T(128)S(1)} %exp.45) | copy-start | bytes 292
  71.1 24.6 %copy-start.56 = (f32[768]{0:T(1024)}, f32[768]{0:T(1024)S(1)}, u32[]{:S(2)}) copy-start(f32[768]{0:T(1024)S(1)} %convert_element_type.168) | copy-start | bytes 9220
  104.8 81.1 %copy-start.40 = (f32[4,24,2]{1,2,0:T(2,128)}, f32[4,24,2]{1,2,0:T(2,128)S(1)}, u32[]{:S(2)}) copy-start(f32[4,24,2]{1,2,0:T(2,128)S(1)} %copy.166) | copy-start | bytes 2308
  105.5 52.3 %copy-start.58 = (f32[2,1,24]{2,1,0:T(1,128)}, f32[2,1,24]{2,1,0:T(1,128)S(1)}, u32[]{:S(2)}) copy-start(f32[2,1,24]{2,1,0:T(1,128)S(1)} %get-tuple-element.318) | copy-start | bytes 580
  105.7 22.6 %copy-start.17 = (f32[4,24,256]{1,0,2:T(4,128)}, f32[4,24,256]{1,0,2:T(4,128)S(1)}, u32[]{:S(2)}) copy-start(f32[4,24,256]{1,0,2:T(4,128)S(1)} %bitcast_multiply_fusion.4) | copy-start | bytes 294916
  107.8 7.6 collective-permute-start.5
  110.5 219.3 %copy-start.49 = (f32[2,24]{1,0:T(2,128)}, f32[2,24]{1,0:T(2,128)S(1)}, u32[]{:S(2)}) copy-start(f32[2,24]{1,0:T(2,128)S(1)} %get-tuple-element.290) | copy-start | bytes 580
  157.8 25.7 %copy-start.38 = (f32[48,768]{1,0:T(8,128)S(1)}, f32[48,768]{1,0:T(8,128)}, u32[]{:S(2)}) copy-start(f32[48,768]{1,0:T(8,128)} %param.28) | copy-start | bytes 442372
  157.8 26.4 %copy-start.69 = (s32[2]{0:T(128)S(1)}, s32[2]{0:T(128)}, u32[]{:S(2)}) copy-start(s32[2]{0:T(128)} %param.19) | copy-start | bytes 28
  158.2 6.2 collective-permute-start.6
  165.8 24.9 %collective-permute-start.7 = (f32[2,24,128,64]{2,3,1,0:T(8,128)}, f32[2,24,128,64]{2,3,1,0:T(8,128)}, u32[]{:S(2)}, u32[]{:S(2)}) collective-permute-start(f32[2,24,128,64]{2,3,1,0:T(8,128)} %multiply_add_fusion.3), channel_id=1, source_target_pairs={{0,1},{1,2},{2,3},{4,5},{5,6},{6,7},{8,9},{9,10},{10,11},{12,13},{... | collective-permute-start | bytes 4718600 | tf_op jit(solution)/shard_map/ppermute | solution.py:48
  184.2 536.0 %reduce-scatter.6.cloned.1.call-start = ((), (), s32[]{:S(2)}) async-start(), calls=%async_computation.4 | async-start | bytes 4866048 | tf_op jit(solution)/shard_map/reduce_scatter | solution.py:335
  184.2 99.1 %copy-start.47 = (f32[1536]{0:T(1024)}, f32[1536]{0:T(1024)S(1)}, u32[]{:S(2)}) copy-start(f32[1536]{0:T(1024)S(1)} %convert_element_type.183) | copy-start | bytes 18436
  184.3 88.4 %copy-start.63 = (f32[2,512]{1,0:T(2,128)}, f32[2,512]{1,0:T(2,128)S(1)}, u32[]{:S(2)}) copy-start(f32[2,512]{1,0:T(2,128)S(1)} %compare_convert_fusion) | copy-start | bytes 12292
  194.0 44.9 %collective-permute-start.8 = (f32[2,24,128,64]{2,3,1,0:T(8,128)}, f32[2,24,128,64]{2,3,1,0:T(8,128)}, u32[]{:S(2)}, u32[]{:S(2)}) collective-permute-start(f32[2,24,128,64]{2,3,1,0:T(8,128)} %multiply_add_fusion.2), channel_id=1, source_target_pairs={{0,1},{1,2},{2,3},{4,5},{5,6},{6,7},{8,9},{9,10},{10,11},{12,13},{... | collective-permute-start | bytes 4718600 | tf_op jit(solution)/shard_map/ppermute | solution.py:48
  323.8 6.0 collective-permute-start.9
  331.2 83.4 %collective-permute-start.10 = (f32[2,24,128,64]{2,3,1,0:T(8,128)}, f32[2,24,128,64]{2,3,1,0:T(8,128)}, u32[]{:S(2)}, u32[]{:S(2)}) collective-permute-start(f32[2,24,128,64]{2,3,1,0:T(8,128)} %multiply_add_fusion.1), channel_id=1, source_target_pairs={{1,0},{2,1},{3,2},{5,4},{6,5},{7,6},{9,8},{10,9},{11,10},{13,12},{... | collective-permute-start | bytes 4718600 | tf_op jit(solution)/shard_map/ppermute | solution.py:48
  414.5 378.2 %reduce-scatter.8.cloned.1.call-start = ((), (), s32[]{:S(2)}) async-start(), calls=%async_computation.5 | async-start | bytes 10948608
  417.9 88.8 %collective-permute-start.11 = (f32[2,24,128,64]{2,3,1,0:T(8,128)}, f32[2,24,128,64]{2,3,1,0:T(8,128)}, u32[]{:S(2)}, u32[]{:S(2)}) collective-permute-start(f32[2,24,128,64]{2,3,1,0:T(8,128)} %multiply_add_fusion), channel_id=1, source_target_pairs={{1,0},{2,1},{3,2},{5,4},{6,5},{7,6},{9,8},{10,9},{11,10},{13,12},{... | collective-permute-start | bytes 4718600 | tf_op jit(solution)/shard_map/ppermute | solution.py:48
  422.6 65.2 %copy-start.37 = (f32[4,24,256]{2,1,0:T(8,128)S(1)}, f32[4,24,256]{2,1,0:T(8,128)}, u32[]{:S(2)}) copy-start(f32[4,24,256]{2,1,0:T(8,128)} %fusion.131) | copy-start | bytes 294916
  626.6 3.6 collective-permute-start.12
  663.4 53.5 %copy-start.15 = (bf16[2,512,768]{2,1,0:T(8,128)(2,1)S(1)}, bf16[2,512,768]{2,1,0:T(8,128)(2,1)}, u32[]{:S(2)}) copy-start(bf16[2,512,768]{2,1,0:T(8,128)(2,1)} %param.18) | copy-start | bytes 4718596
  663.4 53.4 %copy-start.30 = (bf16[2,512,768]{2,1,0:T(8,128)(2,1)S(1)}, bf16[2,512,768]{2,1,0:T(8,128)(2,1)}, u32[]{:S(2)}) copy-start(bf16[2,512,768]{2,1,0:T(8,128)(2,1)} %param.29) | copy-start | bytes 4718596
  663.4 53.4 %copy-start.53 = (f32[2,512]{1,0:T(2,128)S(1)}, f32[2,512]{1,0:T(2,128)}, u32[]{:S(2)}) copy-start(f32[2,512]{1,0:T(2,128)} %get-tuple-element.311) | copy-start | bytes 12292
  (59 other events, 480.4 us)
Sparse Core Ops, SparseCore 0:
  11.5 68.9 all-gather.3
  184.3 56.8 all-gather.5
  414.7 107.2 reduce-scatter.5
  651.5 141.1 reduce-scatter.7
